TPU v7x, 32 devices: a whole 2x2x4 slice. The times are simulated.
32 devices in a mesh: groups: 2 (over x), layer: 4 (over z), iface: 4 (over y, core).
Axes of the slice: x: 2, y: 2, z: 4, core: 2. Of those that a mesh axis runs over, the one named last changes fastest.
Arguments:
- top_trace: bfloat16 [6, 2, 8192, 128], P('groups', None, 'iface'), parts along dimension 0, may hold values from -6 to 6
- sources: bfloat16 [4, 8, 2, 8192, 128], P('layer', 'groups', None, 'iface'), parts along dimension 1, may hold values from -6 to 6
- near_blocks: bfloat16 [4, 2, 32, 8, 256, 256], P('layer', None, 'iface'), may hold values from -0.0625 to 0.0625
- near_index: int32 [32, 8], P('iface'), may hold values from 0 to 31, as said below
- far_left: bfloat16 [4, 2, 64, 8192], P('layer', None, None, 'iface'), may hold values from -0.25 to 0.25
- far_right: bfloat16 [4, 2, 64, 8192], P('layer', None, None, 'iface'), may hold values from -0.046875 to 0.046875
- assign: int32 [4, 3], replicated, may hold values from 0 to 3
Outputs:
- traces: bfloat16 [4, 6, 2, 8192, 128], P('layer', 'groups', None, 'iface'), parts along dimension 1
There are 2 independent parts, one for each index of `groups`. A program takes and returns all parts, laid end to end along the dimension named above; an argument that names none is the same for every part. Nothing has to cross between parts.
Inputs may be any that keep to these rules, and one draw needn't show every extreme that they name: near_index[b, k] = clip(b + o, 0, 8192 / 256 - 1) with the offsets o of a row distinct in -4 .. 4.
All inputs are finite; a program needn't handle non-finite values.
Results may differ from a plain program's by a relative error of at most 0.012.
Values may be sent and summed in bfloat16 or wider, within the bound.
A program may use at most 128 MiB of HBM per device.

v0:
```python
import jax
import jax.numpy as jnp
from jax import lax
from jax.sharding import PartitionSpec as P

BLK = 256
BAND = 4


def passed_along(block, axis, distance):
    devices = range(lax.axis_size(axis))
    route = [(i - distance, i) for i in devices if i - distance in devices]
    return lax.ppermute(block, axis, route)


def per_device(top_trace, sources, near_blocks, near_index, far_left, far_right, assign):
    rows_dev = top_trace.shape[2]
    columns = top_trace.shape[3]
    blocks_dev = rows_dev // BLK
    reach_shards = -(-(BAND * BLK) // rows_dev)
    layer_pos = lax.axis_index("layer")
    panel_count = top_trace.shape[0]
    tick_count = lax.axis_size("layer") + panel_count - 1
    first_block = (lax.axis_index("iface") - reach_shards) * blocks_dev
    local_index = near_index - first_block
    blocks_mat = near_blocks[0]
    left_mat = far_left[0]
    right_mat = far_right[0]
    source_bank = sources[0]

    def neighbours(trace_in):
        below_list = [
            passed_along(trace_in, "iface", offset) for offset in range(reach_shards, 0, -1)
        ]
        above_list = [
            passed_along(trace_in, "iface", -offset) for offset in range(1, reach_shards + 1)
        ]
        return jnp.concatenate(below_list + [trace_in] + above_list, axis=1)

    def mult(mat, vec):
        return jnp.dot(mat, vec, preferred_element_type=jnp.float32)

    def lift(mat, vec):
        return jnp.einsum("ri,rp->ip", mat, vec, preferred_element_type=jnp.float32)

    def propagate(trace_in, panel_idx):
        window = neighbours(trace_in)
        window = window.reshape(2, window.shape[1] // BLK, BLK, columns)
        picked = jnp.take(window, local_index, axis=1)
        part_real = jnp.einsum(
            "jkab,cjkbp->cjap", blocks_mat[0], picked, preferred_element_type=jnp.float32
        )
        part_imag = jnp.einsum(
            "jkab,cjkbp->cjap", blocks_mat[1], picked, preferred_element_type=jnp.float32
        )
        near_term = jnp.stack([part_real[0] - part_imag[1], part_real[1] + part_imag[0]]).reshape(
            2, rows_dev, columns
        )
        partial_value = jnp.stack(
            [
                mult(right_mat[0], trace_in[0]) - mult(right_mat[1], trace_in[1]),
                mult(right_mat[0], trace_in[1]) + mult(right_mat[1], trace_in[0]),
            ]
        )
        coefficient = lax.psum(partial_value, "iface").astype(jnp.bfloat16)
        far_term = jnp.stack(
            [
                lift(left_mat[0], coefficient[0]) - lift(left_mat[1], coefficient[1]),
                lift(left_mat[0], coefficient[1]) + lift(left_mat[1], coefficient[0]),
            ]
        )
        chosen = assign[layer_pos, panel_idx]
        source_term = source_bank[chosen].astype(jnp.float32)
        return (near_term + far_term + source_term).astype(jnp.bfloat16)

    def tick_step(tick_num, carry):
        outgoing, stored = carry
        incoming = passed_along(outgoing, "layer", 1)
        panel_idx = jnp.clip(tick_num - layer_pos, 0, panel_count - 1)
        is_valid = jnp.logical_and(tick_num >= layer_pos, tick_num - layer_pos < panel_count)
        first_trace = top_trace[panel_idx]
        entering = jnp.where(layer_pos == 0, first_trace, incoming)
        updated = propagate(entering, panel_idx)
        previous = stored[0, panel_idx]
        stored = stored.at[0, panel_idx].set(jnp.where(is_valid, updated, previous))
        return (updated, stored)

    outgoing = jnp.zeros((2, rows_dev, columns), jnp.bfloat16)
    stored = jnp.zeros((1,) + top_trace.shape, jnp.bfloat16)
    outgoing, stored = lax.fori_loop(0, tick_count, tick_step, (outgoing, stored))
    return stored


def solution(mesh):
    return jax.shard_map(
        per_device,
        mesh=mesh,
        in_specs=(
            P("groups", None, "iface", None),
            P("layer", "groups", None, "iface", None),
            P("layer", None, "iface", None, None, None),
            P("iface", None),
            P("layer", None, None, "iface"),
            P("layer", None, None, "iface"),
            P(),
        ),
        out_specs=P("layer", "groups", None, "iface", None),
        check_vma=False,
    )
```

profile of v0, /device:TPU:25, one launch (start us, length us, event | category | flops | bytes accessed | tf_op | source)
XLA Modules:
  0.0 694.3 jit_solution(15013799351038586640)
XLA Ops:
  0.7 6.3 copy.22
  9.1 685.2 %while.19 = (s32[]{:T(128)}, bf16[2,2048,128]{1,2,0:T(8,128)(2,1)}, bf16[1,3,2,2048,128]{4,3,2,1,0:T(8,128)(2,1)}, s32[8,8]{1,0:T(8,128)S(1)}, pred[]{:T(512)}, ...) while((s32[]{:T(128)}, bf16[2,2048,128]{1,2,0:T(8,128)(2,1)}, ...), condition=%wide.region_3.4_spmd.clone, body=%wide.region_0.3_spmd.clone.sunk | while | flops 4590716416 | bytes 155688000 | solution.py:90
  18.7 16.5 %collective-permute-done = bf16[2,2048,128]{1,2,0:T(8,128)(2,1)} collective-permute-done((bf16[2,2048,128]{1,2,0:T(8,128)(2,1)S(1)}, bf16[2,2048,128]{1,2,0:T(8,128)(2,1)}, u32[]{:S(2)}, u32[]{:S(2)}) %collective-permute-start) | collective-permute-done | bytes 1048608 | tf_op jit(solution)/shard_map/while/body/eval_jaxpr/ppermute | solution.py:13
  36.5 3.4 collective-permute-start.1
  40.0 3.0 collective-permute-start.2
  44.3 17.1 %psum.15 = bf16[2,64,128]{2,1,0:T(8,128)(2,1)S(1)} all-reduce(f32[2,64,128]{2,1,0:T(8,128)S(1)} %pad_maximum_fusion.5), channel_id=1, replica_groups=mesh['groups'=2,'layer'=4,'iface'=4] {'iface'}, use_global_device_ids=true, to_apply=%region_1.1 | all-reduce | flops 16384 | bytes 98304 | tf_op jit(solution)/shard_map/while/body/eval_jaxpr/psum | solution.py:65
  70.3 3.5 copy.48
  73.8 5.5 gather_fusion
  79.3 9.9 %fusion.81 = f32[2,8,256,128]{2,3,0,1:T(8,128)} fusion(bf16[2,8,8,256,256]{4,3,2,1,0:T(8,128)(2,1)} %get-tuple-element.519, bf16[8,8,2,256,128]{4,3,2,1,0:T(8,128)(2,1)} %bitcast.218, pred[8,8]{1,0:T(8,128)(4,1)S(1)} %compare_and_fusion.2), kind=kOutput, calls=%fused_computation.24.clone.1 | convolution fusion | flops 2151677952 | bytes 18874432 | tf_op jit(solution)/shard_map/while/body/eval_jaxpr/jkab,cjkbp->cjap/dot_general | solution.py:53
  89.2 9.9 %fusion.82 = f32[2,8,256,128]{2,3,0,1:T(8,128)} fusion(bf16[2,8,8,256,256]{4,3,2,1,0:T(8,128)(2,1)} %get-tuple-element.519, bf16[8,8,2,256,128]{4,3,2,1,0:T(8,128)(2,1)} %bitcast.219, pred[8,8]{1,0:T(8,128)(4,1)S(1)} %compare_and_fusion.2), kind=kOutput, calls=%fused_computation.23.clone.1 | convolution fusion | flops 2151677952 | bytes 18874432 | tf_op jit(solution)/shard_map/while/body/eval_jaxpr/jkab,cjkbp->cjap/dot_general | solution.py:50
  110.2 4.0 select_select_fusion.2
  118.8 3.1 fusion.89
  132.7 16.8 %collective-permute-done = bf16[2,2048,128]{1,2,0:T(8,128)(2,1)} collective-permute-done((bf16[2,2048,128]{1,2,0:T(8,128)(2,1)S(1)}, bf16[2,2048,128]{1,2,0:T(8,128)(2,1)}, u32[]{:S(2)}, u32[]{:S(2)}) %collective-permute-start) | collective-permute-done | bytes 1048608 | tf_op jit(solution)/shard_map/while/body/eval_jaxpr/ppermute | solution.py:13
  150.8 3.2 collective-permute-start.1
  154.0 3.5 collective-permute-start.2
  158.8 17.1 %psum.15 = bf16[2,64,128]{2,1,0:T(8,128)(2,1)S(1)} all-reduce(f32[2,64,128]{2,1,0:T(8,128)S(1)} %pad_maximum_fusion.5), channel_id=1, replica_groups=mesh['groups'=2,'layer'=4,'iface'=4] {'iface'}, use_global_device_ids=true, to_apply=%region_1.1 | all-reduce | flops 16384 | bytes 98304 | tf_op jit(solution)/shard_map/while/body/eval_jaxpr/psum | solution.py:65
  184.8 3.5 copy.48
  188.3 5.5 gather_fusion
  193.8 9.9 %fusion.81 = f32[2,8,256,128]{2,3,0,1:T(8,128)} fusion(bf16[2,8,8,256,256]{4,3,2,1,0:T(8,128)(2,1)} %get-tuple-element.519, bf16[8,8,2,256,128]{4,3,2,1,0:T(8,128)(2,1)} %bitcast.218, pred[8,8]{1,0:T(8,128)(4,1)S(1)} %compare_and_fusion.2), kind=kOutput, calls=%fused_computation.24.clone.1 | convolution fusion | flops 2151677952 | bytes 18874432 | tf_op jit(solution)/shard_map/while/body/eval_jaxpr/jkab,cjkbp->cjap/dot_general | solution.py:53
  203.7 9.9 %fusion.82 = f32[2,8,256,128]{2,3,0,1:T(8,128)} fusion(bf16[2,8,8,256,256]{4,3,2,1,0:T(8,128)(2,1)} %get-tuple-element.519, bf16[8,8,2,256,128]{4,3,2,1,0:T(8,128)(2,1)} %bitcast.219, pred[8,8]{1,0:T(8,128)(4,1)S(1)} %compare_and_fusion.2), kind=kOutput, calls=%fused_computation.23.clone.1 | convolution fusion | flops 2151677952 | bytes 18874432 | tf_op jit(solution)/shard_map/while/body/eval_jaxpr/jkab,cjkbp->cjap/dot_general | solution.py:50
  219.1 2.7 copy.52
  224.7 4.0 select_select_fusion.2
  233.3 3.1 fusion.89
  247.2 16.8 %collective-permute-done = bf16[2,2048,128]{1,2,0:T(8,128)(2,1)} collective-permute-done((bf16[2,2048,128]{1,2,0:T(8,128)(2,1)S(1)}, bf16[2,2048,128]{1,2,0:T(8,128)(2,1)}, u32[]{:S(2)}, u32[]{:S(2)}) %collective-permute-start) | collective-permute-done | bytes 1048608 | tf_op jit(solution)/shard_map/while/body/eval_jaxpr/ppermute | solution.py:13
  265.3 3.1 collective-permute-start.1
  268.5 3.5 collective-permute-start.2
  273.2 17.1 %psum.15 = bf16[2,64,128]{2,1,0:T(8,128)(2,1)S(1)} all-reduce(f32[2,64,128]{2,1,0:T(8,128)S(1)} %pad_maximum_fusion.5), channel_id=1, replica_groups=mesh['groups'=2,'layer'=4,'iface'=4] {'iface'}, use_global_device_ids=true, to_apply=%region_1.1 | all-reduce | flops 16384 | bytes 98304 | tf_op jit(solution)/shard_map/while/body/eval_jaxpr/psum | solution.py:65
  299.3 3.5 copy.48
  302.7 5.5 gather_fusion
  308.2 9.9 %fusion.81 = f32[2,8,256,128]{2,3,0,1:T(8,128)} fusion(bf16[2,8,8,256,256]{4,3,2,1,0:T(8,128)(2,1)} %get-tuple-element.519, bf16[8,8,2,256,128]{4,3,2,1,0:T(8,128)(2,1)} %bitcast.218, pred[8,8]{1,0:T(8,128)(4,1)S(1)} %compare_and_fusion.2), kind=kOutput, calls=%fused_computation.24.clone.1 | convolution fusion | flops 2151677952 | bytes 18874432 | tf_op jit(solution)/shard_map/while/body/eval_jaxpr/jkab,cjkbp->cjap/dot_general | solution.py:53
  318.1 9.9 %fusion.82 = f32[2,8,256,128]{2,3,0,1:T(8,128)} fusion(bf16[2,8,8,256,256]{4,3,2,1,0:T(8,128)(2,1)} %get-tuple-element.519, bf16[8,8,2,256,128]{4,3,2,1,0:T(8,128)(2,1)} %bitcast.219, pred[8,8]{1,0:T(8,128)(4,1)S(1)} %compare_and_fusion.2), kind=kOutput, calls=%fused_computation.23.clone.1 | convolution fusion | flops 2151677952 | bytes 18874432 | tf_op jit(solution)/shard_map/while/body/eval_jaxpr/jkab,cjkbp->cjap/dot_general | solution.py:50
  333.5 2.7 copy.52
  339.1 4.0 select_select_fusion.2
  347.8 3.1 fusion.89
  361.7 16.8 %collective-permute-done = bf16[2,2048,128]{1,2,0:T(8,128)(2,1)} collective-permute-done((bf16[2,2048,128]{1,2,0:T(8,128)(2,1)S(1)}, bf16[2,2048,128]{1,2,0:T(8,128)(2,1)}, u32[]{:S(2)}, u32[]{:S(2)}) %collective-permute-start) | collective-permute-done | bytes 1048608 | tf_op jit(solution)/shard_map/while/body/eval_jaxpr/ppermute | solution.py:13
  379.8 3.1 collective-permute-start.1
  383.0 3.5 collective-permute-start.2
  387.7 17.1 %psum.15 = bf16[2,64,128]{2,1,0:T(8,128)(2,1)S(1)} all-reduce(f32[2,64,128]{2,1,0:T(8,128)S(1)} %pad_maximum_fusion.5), channel_id=1, replica_groups=mesh['groups'=2,'layer'=4,'iface'=4] {'iface'}, use_global_device_ids=true, to_apply=%region_1.1 | all-reduce | flops 16384 | bytes 98304 | tf_op jit(solution)/shard_map/while/body/eval_jaxpr/psum | solution.py:65
  413.7 3.5 copy.48
  417.2 5.5 gather_fusion
  422.7 9.9 %fusion.81 = f32[2,8,256,128]{2,3,0,1:T(8,128)} fusion(bf16[2,8,8,256,256]{4,3,2,1,0:T(8,128)(2,1)} %get-tuple-element.519, bf16[8,8,2,256,128]{4,3,2,1,0:T(8,128)(2,1)} %bitcast.218, pred[8,8]{1,0:T(8,128)(4,1)S(1)} %compare_and_fusion.2), kind=kOutput, calls=%fused_computation.24.clone.1 | convolution fusion | flops 2151677952 | bytes 18874432 | tf_op jit(solution)/shard_map/while/body/eval_jaxpr/jkab,cjkbp->cjap/dot_general | solution.py:53
  432.6 9.9 %fusion.82 = f32[2,8,256,128]{2,3,0,1:T(8,128)} fusion(bf16[2,8,8,256,256]{4,3,2,1,0:T(8,128)(2,1)} %get-tuple-element.519, bf16[8,8,2,256,128]{4,3,2,1,0:T(8,128)(2,1)} %bitcast.219, pred[8,8]{1,0:T(8,128)(4,1)S(1)} %compare_and_fusion.2), kind=kOutput, calls=%fused_computation.23.clone.1 | convolution fusion | flops 2151677952 | bytes 18874432 | tf_op jit(solution)/shard_map/while/body/eval_jaxpr/jkab,cjkbp->cjap/dot_general | solution.py:50
  453.6 4.0 select_select_fusion.2
  462.3 3.1 fusion.89
  476.2 16.8 %collective-permute-done = bf16[2,2048,128]{1,2,0:T(8,128)(2,1)} collective-permute-done((bf16[2,2048,128]{1,2,0:T(8,128)(2,1)S(1)}, bf16[2,2048,128]{1,2,0:T(8,128)(2,1)}, u32[]{:S(2)}, u32[]{:S(2)}) %collective-permute-start) | collective-permute-done | bytes 1048608 | tf_op jit(solution)/shard_map/while/body/eval_jaxpr/ppermute | solution.py:13
  494.3 3.1 collective-permute-start.1
  497.4 3.5 collective-permute-start.2
  502.2 17.1 %psum.15 = bf16[2,64,128]{2,1,0:T(8,128)(2,1)S(1)} all-reduce(f32[2,64,128]{2,1,0:T(8,128)S(1)} %pad_maximum_fusion.5), channel_id=1, replica_groups=mesh['groups'=2,'layer'=4,'iface'=4] {'iface'}, use_global_device_ids=true, to_apply=%region_1.1 | all-reduce | flops 16384 | bytes 98304 | tf_op jit(solution)/shard_map/while/body/eval_jaxpr/psum | solution.py:65
  528.2 3.5 copy.48
  531.7 5.5 gather_fusion
  537.2 9.9 %fusion.81 = f32[2,8,256,128]{2,3,0,1:T(8,128)} fusion(bf16[2,8,8,256,256]{4,3,2,1,0:T(8,128)(2,1)} %get-tuple-element.519, bf16[8,8,2,256,128]{4,3,2,1,0:T(8,128)(2,1)} %bitcast.218, pred[8,8]{1,0:T(8,128)(4,1)S(1)} %compare_and_fusion.2), kind=kOutput, calls=%fused_computation.24.clone.1 | convolution fusion | flops 2151677952 | bytes 18874432 | tf_op jit(solution)/shard_map/while/body/eval_jaxpr/jkab,cjkbp->cjap/dot_general | solution.py:53
  547.1 9.9 %fusion.82 = f32[2,8,256,128]{2,3,0,1:T(8,128)} fusion(bf16[2,8,8,256,256]{4,3,2,1,0:T(8,128)(2,1)} %get-tuple-element.519, bf16[8,8,2,256,128]{4,3,2,1,0:T(8,128)(2,1)} %bitcast.219, pred[8,8]{1,0:T(8,128)(4,1)S(1)} %compare_and_fusion.2), kind=kOutput, calls=%fused_computation.23.clone.1 | convolution fusion | flops 2151677952 | bytes 18874432 | tf_op jit(solution)/shard_map/while/body/eval_jaxpr/jkab,cjkbp->cjap/dot_general | solution.py:50
  568.1 4.0 select_select_fusion.2
  576.7 3.1 fusion.89
  590.7 16.8 %collective-permute-done = bf16[2,2048,128]{1,2,0:T(8,128)(2,1)} collective-permute-done((bf16[2,2048,128]{1,2,0:T(8,128)(2,1)S(1)}, bf16[2,2048,128]{1,2,0:T(8,128)(2,1)}, u32[]{:S(2)}, u32[]{:S(2)}) %collective-permute-start) | collective-permute-done | bytes 1048608 | tf_op jit(solution)/shard_map/while/body/eval_jaxpr/ppermute | solution.py:13
  608.8 3.1 collective-permute-start.1
  611.9 3.5 collective-permute-start.2
  616.7 17.1 %psum.15 = bf16[2,64,128]{2,1,0:T(8,128)(2,1)S(1)} all-reduce(f32[2,64,128]{2,1,0:T(8,128)S(1)} %pad_maximum_fusion.5), channel_id=1, replica_groups=mesh['groups'=2,'layer'=4,'iface'=4] {'iface'}, use_global_device_ids=true, to_apply=%region_1.1 | all-reduce | flops 16384 | bytes 98304 | tf_op jit(solution)/shard_map/while/body/eval_jaxpr/psum | solution.py:65
  642.7 3.5 copy.48
  646.2 5.5 gather_fusion
  651.7 9.9 %fusion.81 = f32[2,8,256,128]{2,3,0,1:T(8,128)} fusion(bf16[2,8,8,256,256]{4,3,2,1,0:T(8,128)(2,1)} %get-tuple-element.519, bf16[8,8,2,256,128]{4,3,2,1,0:T(8,128)(2,1)} %bitcast.218, pred[8,8]{1,0:T(8,128)(4,1)S(1)} %compare_and_fusion.2), kind=kOutput, calls=%fused_computation.24.clone.1 | convolution fusion | flops 2151677952 | bytes 18874432 | tf_op jit(solution)/shard_map/while/body/eval_jaxpr/jkab,cjkbp->cjap/dot_general | solution.py:53
  661.6 9.9 %fusion.82 = f32[2,8,256,128]{2,3,0,1:T(8,128)} fusion(bf16[2,8,8,256,256]{4,3,2,1,0:T(8,128)(2,1)} %get-tuple-element.519, bf16[8,8,2,256,128]{4,3,2,1,0:T(8,128)(2,1)} %bitcast.219, pred[8,8]{1,0:T(8,128)(4,1)S(1)} %compare_and_fusion.2), kind=kOutput, calls=%fused_computation.23.clone.1 | convolution fusion | flops 2151677952 | bytes 18874432 | tf_op jit(solution)/shard_map/while/body/eval_jaxpr/jkab,cjkbp->cjap/dot_general | solution.py:50
  682.6 4.0 select_select_fusion.2
  691.2 3.1 fusion.89
  (261 shorter events, 213.4 us)
Async XLA Ops:
  7.0 2.1 copy-start.4
  9.2 26.0 %collective-permute-start = (bf16[2,2048,128]{1,2,0:T(8,128)(2,1)S(1)}, bf16[2,2048,128]{1,2,0:T(8,128)(2,1)}, u32[]{:S(2)}, u32[]{:S(2)}) collective-permute-start(bf16[2,2048,128]{1,2,0:T(8,128)(2,1)S(1)} %broadcast_select_fusion.5), channel_id=1, source_target_pairs={{0,4},{4,8},{8,12},{1,5},{5,9},{9,13},{2,6},{6,10},{10,14},{3,7},{... | collective-permute-start | bytes 3145736 | tf_op jit(solution)/shard_map/while/body/eval_jaxpr/ppermute | solution.py:13
  18.1 25.0 %copy-start.3 = (bf16[2,64,2048]{2,1,0:T(8,128)(2,1)S(1)}, bf16[2,64,2048]{2,1,0:T(8,128)(2,1)}, u32[]{:S(2)}) copy-start(bf16[2,64,2048]{2,1,0:T(8,128)(2,1)} %get-tuple-element.520) | copy-start | bytes 1572868 | tf_op jit(solution)/shard_map/while
  36.5 32.0 %collective-permute-start.1 = (bf16[2,2048,128]{1,2,0:T(8,128)(2,1)S(1)}, bf16[2,2048,128]{1,2,0:T(8,128)(2,1)S(1)}, u32[]{:S(2)}, u32[]{:S(2)}) collective-permute-start(bf16[2,2048,128]{1,2,0:T(8,128)(2,1)S(1)} %bitcast_select_fusion.2), channel_id=1, source_target_pairs={{1,0},{2,1},{3,2},{5,4},{6,5},{7,6},{9,8},{10,9},{11,10},{13,12},{... | collective-permute-start | bytes 3145736 | tf_op jit(solution)/shard_map/while/body/eval_jaxpr/ppermute | solution.py:13
  40.0 28.6 %collective-permute-start.2 = (bf16[2,2048,128]{1,2,0:T(8,128)(2,1)S(1)}, bf16[2,2048,128]{1,2,0:T(8,128)(2,1)S(1)}, u32[]{:S(2)}, u32[]{:S(2)}) collective-permute-start(bf16[2,2048,128]{1,2,0:T(8,128)(2,1)S(1)} %bitcast_select_fusion.2), channel_id=1, source_target_pairs={{0,1},{1,2},{2,3},{4,5},{5,6},{6,7},{8,9},{9,10},{10,11},{12,13},{... | collective-permute-start | bytes 3145736 | tf_op jit(solution)/shard_map/while/body/eval_jaxpr/ppermute | solution.py:13
  104.6 5.6 copy-start
  104.6 5.6 copy-start.1
  114.2 4.6 copy-start.2
  123.2 26.3 %collective-permute-start = (bf16[2,2048,128]{1,2,0:T(8,128)(2,1)S(1)}, bf16[2,2048,128]{1,2,0:T(8,128)(2,1)}, u32[]{:S(2)}, u32[]{:S(2)}) collective-permute-start(bf16[2,2048,128]{1,2,0:T(8,128)(2,1)S(1)} %broadcast_select_fusion.5), channel_id=1, source_target_pairs={{0,4},{4,8},{8,12},{1,5},{5,9},{9,13},{2,6},{6,10},{10,14},{3,7},{... | collective-permute-start | bytes 3145736 | tf_op jit(solution)/shard_map/while/body/eval_jaxpr/ppermute | solution.py:13
  132.1 25.4 %copy-start.3 = (bf16[2,64,2048]{2,1,0:T(8,128)(2,1)S(1)}, bf16[2,64,2048]{2,1,0:T(8,128)(2,1)}, u32[]{:S(2)}) copy-start(bf16[2,64,2048]{2,1,0:T(8,128)(2,1)} %get-tuple-element.520) | copy-start | bytes 1572868 | tf_op jit(solution)/shard_map/while
  150.8 32.2 %collective-permute-start.1 = (bf16[2,2048,128]{1,2,0:T(8,128)(2,1)S(1)}, bf16[2,2048,128]{1,2,0:T(8,128)(2,1)S(1)}, u32[]{:S(2)}, u32[]{:S(2)}) collective-permute-start(bf16[2,2048,128]{1,2,0:T(8,128)(2,1)S(1)} %bitcast_select_fusion.2), channel_id=1, source_target_pairs={{1,0},{2,1},{3,2},{5,4},{6,5},{7,6},{9,8},{10,9},{11,10},{13,12},{... | collective-permute-start | bytes 3145736 | tf_op jit(solution)/shard_map/while/body/eval_jaxpr/ppermute | solution.py:13
  154.0 29.0 %collective-permute-start.2 = (bf16[2,2048,128]{1,2,0:T(8,128)(2,1)S(1)}, bf16[2,2048,128]{1,2,0:T(8,128)(2,1)S(1)}, u32[]{:S(2)}, u32[]{:S(2)}) collective-permute-start(bf16[2,2048,128]{1,2,0:T(8,128)(2,1)S(1)} %bitcast_select_fusion.2), channel_id=1, source_target_pairs={{0,1},{1,2},{2,3},{4,5},{5,6},{6,7},{8,9},{9,10},{10,11},{12,13},{... | collective-permute-start | bytes 3145736 | tf_op jit(solution)/shard_map/while/body/eval_jaxpr/ppermute | solution.py:13
  219.1 5.6 copy-start
  219.1 5.6 copy-start.1
  228.7 4.6 copy-start.2
  237.7 26.3 %collective-permute-start = (bf16[2,2048,128]{1,2,0:T(8,128)(2,1)S(1)}, bf16[2,2048,128]{1,2,0:T(8,128)(2,1)}, u32[]{:S(2)}, u32[]{:S(2)}) collective-permute-start(bf16[2,2048,128]{1,2,0:T(8,128)(2,1)S(1)} %broadcast_select_fusion.5), channel_id=1, source_target_pairs={{0,4},{4,8},{8,12},{1,5},{5,9},{9,13},{2,6},{6,10},{10,14},{3,7},{... | collective-permute-start | bytes 3145736 | tf_op jit(solution)/shard_map/while/body/eval_jaxpr/ppermute | solution.py:13
  246.6 25.4 %copy-start.3 = (bf16[2,64,2048]{2,1,0:T(8,128)(2,1)S(1)}, bf16[2,64,2048]{2,1,0:T(8,128)(2,1)}, u32[]{:S(2)}) copy-start(bf16[2,64,2048]{2,1,0:T(8,128)(2,1)} %get-tuple-element.520) | copy-start | bytes 1572868 | tf_op jit(solution)/shard_map/while
  265.3 32.2 %collective-permute-start.1 = (bf16[2,2048,128]{1,2,0:T(8,128)(2,1)S(1)}, bf16[2,2048,128]{1,2,0:T(8,128)(2,1)S(1)}, u32[]{:S(2)}, u32[]{:S(2)}) collective-permute-start(bf16[2,2048,128]{1,2,0:T(8,128)(2,1)S(1)} %bitcast_select_fusion.2), channel_id=1, source_target_pairs={{1,0},{2,1},{3,2},{5,4},{6,5},{7,6},{9,8},{10,9},{11,10},{13,12},{... | collective-permute-start | bytes 3145736 | tf_op jit(solution)/shard_map/while/body/eval_jaxpr/ppermute | solution.py:13
  268.5 29.0 %collective-permute-start.2 = (bf16[2,2048,128]{1,2,0:T(8,128)(2,1)S(1)}, bf16[2,2048,128]{1,2,0:T(8,128)(2,1)S(1)}, u32[]{:S(2)}, u32[]{:S(2)}) collective-permute-start(bf16[2,2048,128]{1,2,0:T(8,128)(2,1)S(1)} %bitcast_select_fusion.2), channel_id=1, source_target_pairs={{0,1},{1,2},{2,3},{4,5},{5,6},{6,7},{8,9},{9,10},{10,11},{12,13},{... | collective-permute-start | bytes 3145736 | tf_op jit(solution)/shard_map/while/body/eval_jaxpr/ppermute | solution.py:13
  333.5 5.6 copy-start
  333.5 5.6 copy-start.1
  343.1 4.6 copy-start.2
  352.1 26.3 %collective-permute-start = (bf16[2,2048,128]{1,2,0:T(8,128)(2,1)S(1)}, bf16[2,2048,128]{1,2,0:T(8,128)(2,1)}, u32[]{:S(2)}, u32[]{:S(2)}) collective-permute-start(bf16[2,2048,128]{1,2,0:T(8,128)(2,1)S(1)} %broadcast_select_fusion.5), channel_id=1, source_target_pairs={{0,4},{4,8},{8,12},{1,5},{5,9},{9,13},{2,6},{6,10},{10,14},{3,7},{... | collective-permute-start | bytes 3145736 | tf_op jit(solution)/shard_map/while/body/eval_jaxpr/ppermute | solution.py:13
  361.1 25.4 %copy-start.3 = (bf16[2,64,2048]{2,1,0:T(8,128)(2,1)S(1)}, bf16[2,64,2048]{2,1,0:T(8,128)(2,1)}, u32[]{:S(2)}) copy-start(bf16[2,64,2048]{2,1,0:T(8,128)(2,1)} %get-tuple-element.520) | copy-start | bytes 1572868 | tf_op jit(solution)/shard_map/while
  379.8 32.2 %collective-permute-start.1 = (bf16[2,2048,128]{1,2,0:T(8,128)(2,1)S(1)}, bf16[2,2048,128]{1,2,0:T(8,128)(2,1)S(1)}, u32[]{:S(2)}, u32[]{:S(2)}) collective-permute-start(bf16[2,2048,128]{1,2,0:T(8,128)(2,1)S(1)} %bitcast_select_fusion.2), channel_id=1, source_target_pairs={{1,0},{2,1},{3,2},{5,4},{6,5},{7,6},{9,8},{10,9},{11,10},{13,12},{... | collective-permute-start | bytes 3145736 | tf_op jit(solution)/shard_map/while/body/eval_jaxpr/ppermute | solution.py:13
  383.0 29.0 %collective-permute-start.2 = (bf16[2,2048,128]{1,2,0:T(8,128)(2,1)S(1)}, bf16[2,2048,128]{1,2,0:T(8,128)(2,1)S(1)}, u32[]{:S(2)}, u32[]{:S(2)}) collective-permute-start(bf16[2,2048,128]{1,2,0:T(8,128)(2,1)S(1)} %bitcast_select_fusion.2), channel_id=1, source_target_pairs={{0,1},{1,2},{2,3},{4,5},{5,6},{6,7},{8,9},{9,10},{10,11},{12,13},{... | collective-permute-start | bytes 3145736 | tf_op jit(solution)/shard_map/while/body/eval_jaxpr/ppermute | solution.py:13
  448.0 5.6 copy-start
  448.0 5.6 copy-start.1
  457.6 4.6 copy-start.2
  466.6 26.3 %collective-permute-start = (bf16[2,2048,128]{1,2,0:T(8,128)(2,1)S(1)}, bf16[2,2048,128]{1,2,0:T(8,128)(2,1)}, u32[]{:S(2)}, u32[]{:S(2)}) collective-permute-start(bf16[2,2048,128]{1,2,0:T(8,128)(2,1)S(1)} %broadcast_select_fusion.5), channel_id=1, source_target_pairs={{0,4},{4,8},{8,12},{1,5},{5,9},{9,13},{2,6},{6,10},{10,14},{3,7},{... | collective-permute-start | bytes 3145736 | tf_op jit(solution)/shard_map/while/body/eval_jaxpr/ppermute | solution.py:13
  475.5 25.4 %copy-start.3 = (bf16[2,64,2048]{2,1,0:T(8,128)(2,1)S(1)}, bf16[2,64,2048]{2,1,0:T(8,128)(2,1)}, u32[]{:S(2)}) copy-start(bf16[2,64,2048]{2,1,0:T(8,128)(2,1)} %get-tuple-element.520) | copy-start | bytes 1572868 | tf_op jit(solution)/shard_map/while
  494.3 32.2 %collective-permute-start.1 = (bf16[2,2048,128]{1,2,0:T(8,128)(2,1)S(1)}, bf16[2,2048,128]{1,2,0:T(8,128)(2,1)S(1)}, u32[]{:S(2)}, u32[]{:S(2)}) collective-permute-start(bf16[2,2048,128]{1,2,0:T(8,128)(2,1)S(1)} %bitcast_select_fusion.2), channel_id=1, source_target_pairs={{1,0},{2,1},{3,2},{5,4},{6,5},{7,6},{9,8},{10,9},{11,10},{13,12},{... | collective-permute-start | bytes 3145736 | tf_op jit(solution)/shard_map/while/body/eval_jaxpr/ppermute | solution.py:13
  497.4 29.0 %collective-permute-start.2 = (bf16[2,2048,128]{1,2,0:T(8,128)(2,1)S(1)}, bf16[2,2048,128]{1,2,0:T(8,128)(2,1)S(1)}, u32[]{:S(2)}, u32[]{:S(2)}) collective-permute-start(bf16[2,2048,128]{1,2,0:T(8,128)(2,1)S(1)} %bitcast_select_fusion.2), channel_id=1, source_target_pairs={{0,1},{1,2},{2,3},{4,5},{5,6},{6,7},{8,9},{9,10},{10,11},{12,13},{... | collective-permute-start | bytes 3145736 | tf_op jit(solution)/shard_map/while/body/eval_jaxpr/ppermute | solution.py:13
  562.5 5.6 copy-start
  562.5 5.6 copy-start.1
  572.1 4.6 copy-start.2
  581.1 26.3 %collective-permute-start = (bf16[2,2048,128]{1,2,0:T(8,128)(2,1)S(1)}, bf16[2,2048,128]{1,2,0:T(8,128)(2,1)}, u32[]{:S(2)}, u32[]{:S(2)}) collective-permute-start(bf16[2,2048,128]{1,2,0:T(8,128)(2,1)S(1)} %broadcast_select_fusion.5), channel_id=1, source_target_pairs={{0,4},{4,8},{8,12},{1,5},{5,9},{9,13},{2,6},{6,10},{10,14},{3,7},{... | collective-permute-start | bytes 3145736 | tf_op jit(solution)/shard_map/while/body/eval_jaxpr/ppermute | solution.py:13
  590.0 25.4 %copy-start.3 = (bf16[2,64,2048]{2,1,0:T(8,128)(2,1)S(1)}, bf16[2,64,2048]{2,1,0:T(8,128)(2,1)}, u32[]{:S(2)}) copy-start(bf16[2,64,2048]{2,1,0:T(8,128)(2,1)} %get-tuple-element.520) | copy-start | bytes 1572868 | tf_op jit(solution)/shard_map/while
  608.8 32.2 %collective-permute-start.1 = (bf16[2,2048,128]{1,2,0:T(8,128)(2,1)S(1)}, bf16[2,2048,128]{1,2,0:T(8,128)(2,1)S(1)}, u32[]{:S(2)}, u32[]{:S(2)}) collective-permute-start(bf16[2,2048,128]{1,2,0:T(8,128)(2,1)S(1)} %bitcast_select_fusion.2), channel_id=1, source_target_pairs={{1,0},{2,1},{3,2},{5,4},{6,5},{7,6},{9,8},{10,9},{11,10},{13,12},{... | collective-permute-start | bytes 3145736 | tf_op jit(solution)/shard_map/while/body/eval_jaxpr/ppermute | solution.py:13
  611.9 29.0 %collective-permute-start.2 = (bf16[2,2048,128]{1,2,0:T(8,128)(2,1)S(1)}, bf16[2,2048,128]{1,2,0:T(8,128)(2,1)S(1)}, u32[]{:S(2)}, u32[]{:S(2)}) collective-permute-start(bf16[2,2048,128]{1,2,0:T(8,128)(2,1)S(1)} %bitcast_select_fusion.2), channel_id=1, source_target_pairs={{0,1},{1,2},{2,3},{4,5},{5,6},{6,7},{8,9},{9,10},{10,11},{12,13},{... | collective-permute-start | bytes 3145736 | tf_op jit(solution)/shard_map/while/body/eval_jaxpr/ppermute | solution.py:13
  677.0 5.6 copy-start
  677.0 5.6 copy-start.1
  686.6 4.6 copy-start.2
where the time goes:
time: 699 us; the launch traced here: 694 us
  local copies, waits for them, and re-layouts  177 us (25%)
  matrix products  169 us (24%)
  blocking collectives  103 us (15%)
  waiting for transfers between devices  100 us (14%)
  other arithmetic  87 us (12%)
  starting transfers between devices  47.5 us (7%)
  loops' own time  11.4 us (2%)
    psum x6, blocking collectives, propagate(): coefficient = lax.psum(partial_value, 'iface').astype(jnp.bfloat16)  103 us
    ppermute x18, waiting for transfers between devices, passed_along(): return lax.ppermute(block, axis, route)  100 us
    dot_general x6, matrix products, propagate(): jnp.einsum('jkab,cjkbp->cjap', blocks_mat[1], picked, preferred_element_t...  59.5 us
    dot_general x6, matrix products, propagate(): jnp.einsum('jkab,cjkbp->cjap', blocks_mat[0], picked, preferred_element_t...  59.3 us
    ppermute x18, starting transfers between devices, passed_along(): return lax.ppermute(block, axis, route)  47.5 us
    dot_general x24, matrix products, lift(): return jnp.einsum('ri,rp->ip', mat, vec, preferred_element_type=jnp.float32)  42.5 us
    another operation x24, local copies, waits for them, and re-layouts, propagate(): jnp.stack([part_real[0] - part_imag[1], part_real[1] + part_imag[0]])  41.6 us
    gather x6, local copies, waits for them, and re-layouts, propagate(): picked = jnp.take(window, local_index, axis=1)  32.9 us
  transfers between devices with their start and end apart: 18, of which 6 were waited for; matrix products, arithmetic and copies ran while one was open for 13% of the time, Pallas kernels for 0%

commit v1 on v0

v1 whole, which is shorter than its diff:
```python
import functools

import jax
import jax.numpy as jnp
from jax import lax
from jax.experimental import pallas as pl
from jax.experimental.pallas import tpu as pltpu
from jax.sharding import PartitionSpec as P

BLK = 256
BAND = 4
MESH = pl.DeviceIdType.MESH


def times_i(value):
    half = value.shape[1] // 2
    rolled = pltpu.roll(value, half, 1)
    lane = lax.broadcasted_iota(jnp.int32, value.shape, 1)
    return jnp.where(lane < half, -rolled, rolled)


def halo_list(blocks_dev):
    reach = -(-BAND // blocks_dev)
    pairs = []
    for j in range(blocks_dev):
        for d in range(1, reach + 1):
            if j >= d * blocks_dev - BAND:
                pairs.append((j, d, j - d * blocks_dev + BAND))
            if j < blocks_dev - d * blocks_dev + BAND:
                pairs.append((j, -d, j + d * blocks_dev + BAND))
    return pairs


def kernel(
    n_iface, n_layer, chunks, blocks_dev, near_count, rank,
    index_ref, top_ref, source_ref, near_hbm, left_ref, right_ref,
    out_ref,
    win, work, near, ucat, coef, ccat,
    z_send, z_recv, h_send, h_recv, f_send, f_recv, top_sem, near_sem,
):
    me = lax.axis_index("iface")
    layer = lax.axis_index("layer")
    halos = halo_list(blocks_dev)
    reach = -(-BAND // blocks_dev)
    has_up = layer > 0
    has_down = layer < n_layer - 1

    def top_copy(t):
        return pltpu.make_async_copy(
            top_ref.at[t], win.at[t, pl.ds(BAND, blocks_dev)], top_sem.at[t]
        )

    def near_copy(j, k):
        return pltpu.make_async_copy(
            near_hbm.at[:, j, k], near.at[:, j, :, pl.ds(k * BLK, BLK)], near_sem.at[j, k]
        )

    def z_copy(t, j):
        return pltpu.make_async_remote_copy(
            src_ref=out_ref.at[t, j],
            dst_ref=win.at[t, BAND + j],
            send_sem=z_send.at[t, j],
            recv_sem=z_recv.at[t, j],
            device_id={"layer": layer + 1},
            device_id_type=MESH,
        )

    def h_copy(t, q):
        j, d, place = halos[q]
        return pltpu.make_async_remote_copy(
            src_ref=win.at[t, BAND + j],
            dst_ref=win.at[t, place],
            send_sem=h_send.at[t, q],
            recv_sem=h_recv.at[t, q],
            device_id={"iface": me + d},
            device_id_type=MESH,
        )

    def inside(pos):
        return jnp.logical_and(pos >= 0, pos < n_iface)

    def f_copy(t, d):
        return pltpu.make_async_remote_copy(
            src_ref=coef.at[t, 0],
            dst_ref=coef.at[t, d],
            send_sem=f_send.at[t, d],
            recv_sem=f_recv.at[t, d],
            device_id={"iface": lax.rem(me + d, n_iface)},
            device_id_type=MESH,
        )

    @pl.when(layer == 0)
    def _():
        for t in range(chunks):
            top_copy(t).start()

    for j in range(blocks_dev):
        for k in range(near_count):
            near_copy(j, k).start()

    barrier = pltpu.get_barrier_semaphore()
    for d in range(1, n_iface):
        pl.semaphore_signal(
            barrier, inc=1, device_id={"iface": lax.rem(me + d, n_iface)}, device_id_type=MESH
        )

    @pl.when(has_up)
    def _():
        pl.semaphore_signal(
            barrier, inc=1, device_id={"layer": layer - 1}, device_id_type=MESH
        )

    @pl.when(has_down)
    def _():
        pl.semaphore_signal(
            barrier, inc=1, device_id={"layer": layer + 1}, device_id_type=MESH
        )

    neighbours = jnp.where(has_up, 1, 0) + jnp.where(has_down, 1, 0)
    pl.semaphore_wait(barrier, n_iface - 1 + neighbours)

    def chunk_step(t, carry):
        @pl.when(layer == 0)
        def _():
            top_copy(t).wait()

        partial = None
        for j in range(blocks_dev):
            @pl.when(has_up)
            def _():
                z_copy(t, j).wait_recv()

            for q, (hj, d, _place) in enumerate(halos):
                if hj == j:
                    @pl.when(inside(me + d))
                    def _():
                        h_copy(t, q).start()

            term = jnp.dot(
                right_ref[:, j * BLK : (j + 1) * BLK],
                win[t, BAND + j],
                preferred_element_type=jnp.float32,
            )
            partial = term if partial is None else partial + term
        coef[t, 0] = partial[:rank] + times_i(partial[rank:])
        for d in range(1, n_iface):
            f_copy(t, d).start()

        for q, (_j, d, _place) in enumerate(halos):
            @pl.when(inside(me - d))
            def _():
                h_copy(t, q).wait_recv()

        work[...] = win[t]
        for d in range(1, n_iface):
            f_copy(t, d).wait_recv()
        total = coef[t, 0]
        for d in range(1, n_iface):
            total = total + coef[t, d]
        total = total.astype(jnp.bfloat16)
        ccat[0:rank] = total
        ccat[rank : 2 * rank] = times_i(total.astype(jnp.float32)).astype(jnp.bfloat16)

        def row_step(j, inner):
            @pl.when(t == 0)
            def _():
                for k in range(near_count):
                    near_copy(j, k).wait()

            for k in range(near_count):
                ucat[k * BLK : (k + 1) * BLK] = work[index_ref[j, k]]
            pieces = []
            for c in range(2):
                pieces.append(
                    jnp.dot(near[c, j], ucat[...], preferred_element_type=jnp.float32)
                )
            far = jnp.dot(left_ref[j], ccat[...], preferred_element_type=jnp.float32)
            result = pieces[0] + times_i(pieces[1]) + far + source_ref[t, j].astype(jnp.float32)
            out_ref[t, j] = result.astype(jnp.bfloat16)

            @pl.when(has_down)
            def _():
                z_copy(t, j).start()

            return inner

        return lax.fori_loop(0, blocks_dev, row_step, carry)

    lax.fori_loop(0, chunks, chunk_step, 0)

    def drain(t, carry):
        for q, (_j, d, _place) in enumerate(halos):
            @pl.when(inside(me + d))
            def _():
                h_copy(t, q).wait_send()

        for d in range(1, n_iface):
            f_copy(t, d).wait_send()

        @pl.when(has_down)
        def _():
            for j in range(blocks_dev):
                z_copy(t, j).wait_send()

        return carry

    lax.fori_loop(0, chunks, drain, 0)


def packed(array):
    panels, _, rows, columns = array.shape
    half = columns // 2
    parts = [
        jnp.concatenate(
            [array[:, 0, :, h * half : (h + 1) * half], array[:, 1, :, h * half : (h + 1) * half]],
            axis=-1,
        )
        for h in range(2)
    ]
    return jnp.stack(parts, axis=1).reshape(panels * 2, rows // BLK, BLK, columns)


def unpacked(array, panels):
    _, blocks, _, columns = array.shape
    half = columns // 2
    array = array.reshape(panels, 2, blocks * BLK, columns)
    parts = [
        jnp.concatenate(
            [array[:, 0, :, c * half : (c + 1) * half], array[:, 1, :, c * half : (c + 1) * half]],
            axis=-1,
        )
        for c in range(2)
    ]
    return jnp.stack(parts, axis=1)


def per_device(n_iface, n_layer, top_trace, sources, near_blocks, near_index, far_left, far_right, assign):
    panels, _, rows_dev, columns = top_trace.shape
    blocks_dev = rows_dev // BLK
    near_count = near_index.shape[1]
    rank = far_left.shape[2]
    chunks = panels * 2
    layer_pos = lax.axis_index("layer")
    local_index = near_index - (lax.axis_index("iface") * blocks_dev - BAND)
    chosen = jnp.take(sources[0], assign[layer_pos], axis=0)
    top = packed(top_trace)
    source = packed(chosen)
    left = far_left[0].reshape(2 * rank, rows_dev).T.reshape(blocks_dev, BLK, 2 * rank)
    right = far_right[0].reshape(2 * rank, rows_dev)
    halo_count = len(halo_list(blocks_dev))
    window = blocks_dev + 2 * BAND
    vmem = pl.BlockSpec(memory_space=pltpu.VMEM)
    anywhere = pl.BlockSpec(memory_space=pl.ANY)
    dma = pltpu.SemaphoreType.DMA
    bf16 = jnp.bfloat16
    out = pl.pallas_call(
        functools.partial(kernel, n_iface, n_layer, chunks, blocks_dev, near_count, rank),
        out_shape=jax.ShapeDtypeStruct((chunks, blocks_dev, BLK, columns), bf16),
        in_specs=[
            pl.BlockSpec(memory_space=pltpu.SMEM), anywhere, vmem, anywhere, vmem, vmem,
        ],
        out_specs=vmem,
        scratch_shapes=[
            pltpu.VMEM((chunks, window, BLK, columns), bf16),
            pltpu.VMEM((window, BLK, columns), bf16),
            pltpu.VMEM((2, blocks_dev, BLK, near_count * BLK), bf16),
            pltpu.VMEM((near_count * BLK, columns), bf16),
            pltpu.VMEM((chunks, n_iface, rank, columns), jnp.float32),
            pltpu.VMEM((2 * rank, columns), bf16),
            dma((chunks, blocks_dev)),
            dma((chunks, blocks_dev)),
            dma((chunks, halo_count)),
            dma((chunks, halo_count)),
            dma((chunks, n_iface)),
            dma((chunks, n_iface)),
            dma((chunks,)),
            dma((blocks_dev, near_count)),
        ],
        compiler_params=pltpu.CompilerParams(collective_id=0, has_side_effects=True),
    )(local_index, top, source, near_blocks[0], left, right)
    return unpacked(out, panels)[None]


def solution(mesh):
    return jax.shard_map(
        functools.partial(per_device, mesh.shape["iface"], mesh.shape["layer"]),
        mesh=mesh,
        in_specs=(
            P("groups", None, "iface", None),
            P("layer", "groups", None, "iface", None),
            P("layer", None, "iface", None, None, None),
            P("iface", None),
            P("layer", None, None, "iface"),
            P("layer", None, None, "iface"),
            P(),
        ),
        out_specs=P("layer", "groups", None, "iface", None),
        check_vma=False,
    )
```

time: 699 us -> 163 us (0.23)
  matrix products: 169 us -> 0 us
  local copies, waits for them, and re-layouts: 177 us -> 15.6 us
  Pallas kernels: 0 us -> 137 us
  blocking collectives: 103 us -> 0 us
  waiting for transfers between devices: 100 us -> 0 us
  other arithmetic: 87 us -> 10 us
  starting transfers between devices: 47.5 us -> 0 us
  loops' own time: 11.4 us -> 0 us
    dot_general x60 -> x0, matrix products: 169 us -> none  [the longest x6 59.5 us: propagate(): jnp.einsum('jkab,cjkbp->cjap', blocks_mat[1], picked, preferred_element_t...]
    pallas_call x0 -> x1, Pallas kernels: none -> 137 us  [per_device(): pl.pallas_call(functools.partial(kernel, n_iface, n_layer, chunks, blocks...]
    psum x6 -> x0, blocking collectives: 103 us -> none  [propagate(): coefficient = lax.psum(partial_value, 'iface').astype(jnp.bfloat16)]
    ppermute x18 -> x0, waiting for transfers between devices: 100 us -> none  [passed_along(): return lax.ppermute(block, axis, route)]
    ppermute x18 -> x0, starting transfers between devices: 47.5 us -> none  [passed_along(): return lax.ppermute(block, axis, route)]
    another operation x30 -> x3, local copies, waits for them, and re-layouts: 42.1 us -> 4.74 us  [the longest x2 3.72 us: packed(): jnp.stack(parts, axis=1).reshape(panels * 2, rows // BLK, BLK, columns)]
    dynamic_slice x30 -> x0, local copies, waits for them, and re-layouts: 34.2 us -> none  [the longest x12 15.7 us: tick_step(): previous = stored[0, panel_idx]]
    gather x6 -> x1, local copies, waits for them, and re-layouts: 32.9 us -> 3.34 us  [per_device(): chosen = jnp.take(sources[0], assign[layer_pos], axis=0)]
  transfers between devices with their start and end apart: 18 -> 0, of which waited for: 6 -> 0; matrix products, arithmetic and copies ran while one was open for 13% -> 0% of each run, Pallas kernels for 0% -> 0%
where the time goes in v1:
time: 163 us
  Pallas kernels  137 us (84%)
  local copies, waits for them, and re-layouts  15.6 us (10%)
  other arithmetic  10 us (6%)
    pallas_call x1, Pallas kernels, per_device(): pl.pallas_call(functools.partial(kernel, n_iface, n_layer, chunks, blocks...  137 us
    squeeze x1, local copies, waits for them, and re-layouts, unpacked(): array[:, 0, :, c * half:(c + 1) * half]  4.2 us
    another operation x4, other arithmetic, packed(): jnp.stack(parts, axis=1).reshape(panels * 2, rows // BLK, BLK, columns)  4.03 us
    another operation x2, local copies, waits for them, and re-layouts, packed(): jnp.stack(parts, axis=1).reshape(panels * 2, rows // BLK, BLK, columns)  3.72 us
    gather x1, local copies, waits for them, and re-layouts, per_device(): chosen = jnp.take(sources[0], assign[layer_pos], axis=0)  3.34 us

profile of v1, /device:TPU:25, one launch (start us, length us, event | category | flops | bytes accessed | tf_op | source)
XLA Modules:
  0.0 163.0 jit_solution(9622211047694742875)
XLA Ops:
  0.0 0.7 fusion
  0.7 3.3 %gather_fusion = bf16[3,2,2048,128]{3,2,1,0:T(8,128)(2,1)S(1)} fusion(bf16[4,2,2048,128]{3,2,1,0:T(8,128)(2,1)} %bitcast.78, s32[1024]{0:T(1024)S(1)} %pad_clamp_fusion), kind=kCustom, calls=%fused_computation | custom fusion | bytes 6291468 | tf_op jit(solution)/shard_map/jit(_take)/gather | solution.py:245
  4.0 0.7 compare_and_fusion
  4.7 0.4 broadcast_select_fusion
  5.1 1.1 slice_bitcast_fusion.7
  6.2 1.7 %maximum_bitcast_fusion.3 = (bf16[3,1,2048,128]{3,2,0,1:T(8,128)(2,1)S(1)}, bf16[3,1,2048,128]{3,2,0,1:T(8,128)(2,1)S(1)}) fusion(bf16[3,2048,64]{2,1,0:T(8,128)(2,1)S(1)} %get-tuple-element.10, bf16[3,2048,64]{2,1,0:T(8,128)(2,1)S(1)} %get-tuple-element.9, bf16[3,2048,64]{2,1,0:T(8,128)(2,1)S(1)} %get-tuple-element.11, ...), kind=kLoop, calls=%fused_computation.15 | loop fusion | flops 6291456 | bytes 6291456 | tf_op jit(solution)/shard_map/stack | solution.py:220
  7.9 0.3 pad_maximum_fusion.1
  8.2 0.0 copy-start
  8.3 1.8 %copy.15 = bf16[3,2,2048,128]{3,2,1,0:T(8,128)(2,1)} copy(bf16[3,2,2048,128]{3,2,0,1:T(8,128)(2,1)S(1)} %pad_maximum_fusion.1) | data formatting | bytes 6291456 | tf_op jit(solution)/shard_map/stack | solution.py:220
  10.1 1.2 copy-done
  11.3 1.1 slice_bitcast_fusion.11
  12.4 1.7 %maximum_bitcast_fusion.1 = (bf16[3,1,2048,128]{3,2,0,1:T(8,128)(2,1)S(1)}, bf16[3,1,2048,128]{3,2,0,1:T(8,128)(2,1)S(1)}) fusion(bf16[3,2048,64]{2,1,0:T(8,128)(2,1)S(1)} %get-tuple-element.16, bf16[3,2048,64]{2,1,0:T(8,128)(2,1)S(1)} %get-tuple-element.13, bf16[3,2048,64]{2,1,0:T(8,128)(2,1)S(1)} %get-tuple-element.15, ...), kind=kLoop, calls=%fused_computation.13 | loop fusion | flops 6291456 | bytes 6291456 | tf_op jit(solution)/shard_map/stack | solution.py:220
  14.1 0.3 pad_maximum_fusion
  14.4 0.0 copy-start.2
  14.4 0.0 copy-start.1
  14.4 1.9 %copy.11 = bf16[3,2,2048,128]{3,2,1,0:T(8,128)(2,1)} copy(bf16[3,2,2048,128]{3,2,0,1:T(8,128)(2,1)S(1)} %pad_maximum_fusion) | data formatting | bytes 6291456 | tf_op jit(solution)/shard_map/stack | solution.py:220
  16.3 0.0 copy-done.2
  16.3 0.6 broadcast_subtract_fusion.index_ref
  16.9 0.0 copy-done.1
  16.9 1.0 copy.16
  17.9 137.2 %shard_map.73 = bf16[6,8,256,128]{3,2,1,0:T(8,128)(2,1)} custom-call(s32[8,8]{1,0:T(8,128)} %broadcast_subtract_fusion.index_ref, bf16[6,8,256,128]{3,2,1,0:T(8,128)(2,1)} %bitcast.77, bf16[6,8,256,128]{3,2,1,0:T(8,128)(2,1)} %bitcast.76, bf16[2,8,8,256,256]{4,3,2,1,0:T(8,128)(2,1)} %bitcast.75, bf16[8,256,128]{2,1,0:T(8,128)(2,1)} %bitcast.79, ...), custom_call_target="tpu_custom_call" | custom-call | tf_op jit(solution)/shard_map/pallas_call | solution.py:256
  155.1 4.2 %slice_bitcast_fusion.3 = (bf16[3,2048,64]{2,1,0:T(8,128)(2,1)S(1)}, bf16[3,2048,64]{2,1,0:T(8,128)(2,1)S(1)}, bf16[3,2048,64]{2,1,0:T(8,128)(2,1)S(1)}, bf16[3,2048,64]{2,1,0:T(8,128)(2,1)S(1)}) fusion(bf16[3,2,2048,128]{3,2,1,0:T(8,128)(2,1)} %bitcast.74), kind=kLoop, calls=%fused_computation.8 | loop fusion | bytes 6291456 | tf_op jit(solution)/shard_map/squeeze | solution.py:229
  159.3 0.9 maximum_bitcast_fusion.5
  160.2 0.9 maximum_bitcast_fusion.6
  161.0 1.9 %maximum_bitcast_fusion = bf16[1,3,2,2048,128]{4,3,2,1,0:T(8,128)(2,1)} fusion(bf16[3,1,2048,128]{3,2,1,0:T(8,128)(2,1)S(1)} %maximum_bitcast_fusion.6, bf16[3,1,2048,128]{3,2,1,0:T(8,128)(2,1)S(1)} %maximum_bitcast_fusion.5), kind=kLoop, calls=%fused_computation.3 | loop fusion | flops 1572864 | bytes 6291456 | tf_op jit(solution)/shard_map/broadcast_in_dim | solution.py:281
  (1 shorter events, 0.0 us)
Async XLA Ops:
  8.2 3.0 %copy-start = (bf16[3,2,2048,128]{3,2,1,0:T(8,128)(2,1)S(1)}, bf16[3,2,2048,128]{3,2,1,0:T(8,128)(2,1)}, u32[]{:S(2)}) copy-start(bf16[3,2,2048,128]{3,2,1,0:T(8,128)(2,1)} %param.7) | copy-start | bytes 9437188
  14.4 1.9 %copy-start.2 = (s32[8,8]{1,0:T(8,128)S(1)}, s32[8,8]{1,0:T(8,128)}, u32[]{:S(2)}) copy-start(s32[8,8]{1,0:T(8,128)} %param.10) | copy-start | bytes 772
  14.4 2.5 %copy-start.1 = (bf16[1,2,64,2048]{3,2,1,0:T(8,128)(2,1)S(1)}, bf16[1,2,64,2048]{3,2,1,0:T(8,128)(2,1)}, u32[]{:S(2)}) copy-start(bf16[1,2,64,2048]{3,2,1,0:T(8,128)(2,1)} %param.11) | copy-start | bytes 1572868
